TPU v7x, 256 devices: a whole 4x4x8 slice. The times are simulated.
256 devices in a mesh: wide: 32 (over y, x, core), narrow: 8 (over z).
Axes of the slice: x: 4, y: 4, z: 8, core: 2. Of those that a mesh axis runs over, the one named last changes fastest.
Arguments:
- thinker_rows: bfloat16 [32, 8, 3, 2, 128, 2048], P('wide', 'narrow'), may hold values from -6 to 6
- codec_ids: int32 [32, 8, 3, 2, 128], P('wide', 'narrow'), may hold values from 0 to 2047
- block_lengths: int32 [32, 8, 3, 2], P('wide', 'narrow'), may hold values from 1 to 128
- chosen_label: int32 [32, 8, 3], P('wide', 'narrow'), may hold values from 0 to 1
- ref_logratio: float32 [32, 8, 3], P('wide', 'narrow'), may hold values from -6 to 6
- pair_count: int32 [32, 8], P('wide', 'narrow'), may hold values from 1 to 3, as said below
- proj_weight: bfloat16 [2048, 1024], P('narrow'), may hold values from -0.125 to 0.125
- norm_gain: bfloat16 [1024], P('narrow'), may hold values from 0.25 to 1.75
- head_weight: bfloat16 [1024, 2048], P('narrow')
Outputs:
- loss: float32 [], replicated
- grad_head: float32 [1024, 2048], P('narrow')
- grad_gain: float32 [1024], P('narrow')
Inputs may be any that keep to these rules, and one draw needn't show every extreme that they name: `pair_count`: owners are ordered with the wide index slowest; the counts sum to 512; the sum of the counts of owners below owner i lies between i * 2 and i * 2 + 1; some owner holds 3 live pairs.
All inputs are finite; a program needn't handle non-finite values.
Results may differ from a plain program's by a relative error of at most 0.017.
The roundings to bfloat16 on the way count: a program that leaves them out, or rounds other values in their place, can miss the bound.
Values may be sent and summed in bfloat16 or wider, within the bound.
No kernel may reach another device: no remote copies, remote signals or barrier semaphores. Data moves between devices by JAX's collectives and lax.ppermute only.
A program may use at most 64 MiB of HBM per device.

v0:
```python
import jax
import jax.numpy as jnp
from jax import lax
from jax.sharding import PartitionSpec as P

norm_eps = 1e-06
margin_scale = 2.0


def forward_terms(projected, codes, lengths, live_pairs, gain_full, head_full):
    pairs = codes.shape[0]
    frames = codes.shape[2]
    flat = projected.astype(jnp.float32)
    inverse = lax.rsqrt(jnp.mean(flat * flat, axis=1, keepdims=True) + norm_eps)
    normed = (flat * inverse * gain_full.astype(jnp.float32)).astype(jnp.bfloat16)
    logits = jnp.dot(normed, head_full, preferred_element_type=jnp.float32)
    highest = jnp.max(logits, axis=1, keepdims=True)
    log_total = highest + jnp.log(jnp.sum(jnp.exp(logits - highest), axis=1, keepdims=True))
    probs = jnp.exp(logits - log_total)
    target = (lax.broadcasted_iota(jnp.int32, logits.shape, 1) == codes.reshape(-1, 1)).astype(
        jnp.float32
    )
    token_logp = jnp.sum(target * logits, axis=1) - log_total[:, 0]
    frame_index = jnp.arange(frames, dtype=jnp.int32)
    valid = ((frame_index[None, None, :] < lengths[:, :, None]) & live_pairs[:, None, None]).astype(
        jnp.float32
    )
    partial_value = jnp.sum(token_logp.reshape(pairs, 2, frames) * valid, axis=2)
    return (normed, flat, inverse, probs, target, valid, partial_value)


def backward_terms(
    scores, lengths, labels, ratios, live_pairs, flat, inverse, probs, target, valid, head_full
):
    length_f = lengths.astype(jnp.float32)
    score = scores / length_f
    first = labels == 0
    chosen = jnp.where(first, score[:, 0], score[:, 1])
    rejected = jnp.where(first, score[:, 1], score[:, 0])
    margin = margin_scale * (chosen - rejected - ratios)
    live_f = live_pairs.astype(jnp.float32)
    loss_part = jnp.sum(jax.nn.softplus(-margin) * live_f)
    slope = -jax.nn.sigmoid(-margin) * live_f
    weight_first = jnp.where(first, margin_scale * slope, -margin_scale * slope)
    block_weight = jnp.stack([weight_first, -weight_first], axis=1) / length_f
    coeff = (block_weight[:, :, None] * valid).reshape(-1, 1)
    dlogits = (coeff * (target - probs)).astype(jnp.bfloat16)
    dnormed = jnp.dot(dlogits, head_full.T, preferred_element_type=jnp.float32)
    gain_term = jnp.sum(dnormed * flat * inverse, axis=0)
    return (loss_part, dlogits, gain_term)


def on_device(
    thinker_rows,
    codec_ids,
    block_lengths,
    chosen_label,
    ref_logratio,
    pair_count,
    proj_weight,
    norm_gain,
    head_weight,
):
    slots = thinker_rows.shape[2]
    frames = thinker_rows.shape[4]
    thinker_width = thinker_rows.shape[5]
    width = proj_weight.shape[1]
    hold = (slots + 1) // 2
    wide_count = lax.axis_size("wide")
    narrow_count = lax.axis_size("narrow")
    flat_rows = thinker_rows.reshape(slots * 2 * frames, thinker_width)
    projected = jnp.dot(
        flat_rows,
        lax.all_gather(proj_weight, "narrow", axis=0, tiled=True),
        preferred_element_type=jnp.float32,
    ).astype(jnp.bfloat16)
    head_full, gain_full = (
        lax.all_gather(head_weight, "narrow", axis=0, tiled=True),
        lax.all_gather(norm_gain, "narrow", axis=0, tiled=True),
    )
    codes = codec_ids[0, 0]
    lengths = block_lengths[0, 0]
    labels = chosen_label[0, 0]
    ratios = ref_logratio[0, 0]
    live_pairs = jnp.arange(slots, dtype=jnp.int32) < pair_count[0, 0]
    normed, flat, inverse, probs, target, valid, partial_value = forward_terms(
        projected, codes, lengths, live_pairs, gain_full, head_full
    )
    loss_part, dlogits, gain_term = backward_terms(
        partial_value,
        lengths,
        labels,
        ratios,
        live_pairs,
        flat,
        inverse,
        probs,
        target,
        valid,
        head_full,
    )
    pair_total = wide_count * narrow_count * hold
    loss_sum = lax.psum(loss_part, ("wide", "narrow"))
    block = width // (wide_count * narrow_count)
    row_count = normed.shape[0]
    normed_order = (
        normed.reshape(row_count, narrow_count, wide_count, block)
        .transpose(0, 2, 1, 3)
        .reshape(row_count, width)
    )
    head_order = jnp.dot(normed_order.T, dlogits, preferred_element_type=jnp.float32)
    gain_order = (
        gain_term.reshape(narrow_count, wide_count, block).transpose(1, 0, 2).reshape(width)
    )
    head_piece, gain_piece = (
        lax.psum_scatter(head_order, ("wide", "narrow"), scatter_dimension=0, tiled=True),
        lax.psum_scatter(gain_order, ("wide", "narrow"), scatter_dimension=0, tiled=True),
    )
    grad_head, grad_gain = (
        lax.all_gather(head_piece.astype(jnp.bfloat16), "wide", axis=0, tiled=True).astype(
            head_piece.dtype
        ),
        lax.all_gather(gain_piece.astype(jnp.bfloat16), "wide", axis=0, tiled=True).astype(
            gain_piece.dtype
        ),
    )
    return (loss_sum / pair_total, grad_head, grad_gain)


def solution(mesh):
    in_specs = (
        P("wide", "narrow", None, None, None, None),
        P("wide", "narrow", None, None, None),
        P("wide", "narrow", None, None),
        P("wide", "narrow", None),
        P("wide", "narrow", None),
        P("wide", "narrow"),
        P("narrow", None),
        P("narrow"),
        P("narrow", None),
    )
    out_specs = (P(), P("narrow", None), P("narrow"))
    return jax.shard_map(
        on_device, mesh=mesh, in_specs=in_specs, out_specs=out_specs, check_vma=False
    )
```

profile of v0, /device:TPU:1, one launch (start us, length us, event | category | flops | bytes accessed | tf_op | source)
XLA Modules:
  0.0 399.8 jit_solution(17206909398932565671)
XLA Ops:
  7.2 0.7 all-gather.5.cloned.1.call-update
  8.0 0.7 all-gather.7.cloned.1.call-update
  9.3 0.7 compare_bitcast_fusion
  10.1 0.8 copy.33
  10.9 0.7 copy.39
  11.6 0.7 eq.29
  12.3 16.4 %all-gather = bf16[8,1,128]{2,1,0:T(2,128)(2,1)S(1)} all-gather(bf16[1,1,128]{2,1,0:T(2,128)(2,1)} %bitcast.53), channel_id=1, replica_groups=mesh['wide'=32,'narrow'=8] {'narrow'}, dimensions={0}, use_global_device_ids=true | all-gather | bytes 2304 | tf_op jit(solution)/shard_map/all_gather | solution.py:79
  28.7 1.3 dynamic-slice
  29.9 38.3 %all-gather.5.cloned.1.call-done = bf16[2048,1024]{1,0:T(8,128)(2,1)} async-done(((bf16[256,1024]{1,0:T(8,128)(2,1)}), bf16[2048,1024]{1,0:T(8,128)(2,1)}) %all-gather.5.cloned.1.call-update) | async-done | bytes 4194320 | tf_op jit(solution)/shard_map/all_gather | solution.py:74
  68.2 5.7 %fusion = (f32[768]{0:T(1024)S(1)}, bf16[768,1024]{1,0:T(8,128)(2,1)S(1)}) fusion(bf16[768,2048]{1,0:T(8,128)(2,1)S(1)} %bitcast.47, bf16[2048,1024]{1,0:T(8,128)(2,1)} %all-gather.5.cloned.1.call-done), kind=kOutput, calls=%fused_computation.7 | convolution fusion | flops 3224370432 | bytes 8915968 | tf_op jit(solution)/shard_map/dot_general | solution.py:72
  73.9 1.1 copy-done.3
  75.0 1.6 fusion.2
  76.6 2.6 copy.35
  79.2 3.9 reshape.130
  83.1 3.4 copy.36
  86.5 3.8 reshape.131
  90.3 33.1 %all-gather.7.cloned.1.call-done = bf16[1024,2048]{1,0:T(8,128)(2,1)} async-done(((bf16[128,2048]{1,0:T(8,128)(2,1)}), bf16[1024,2048]{1,0:T(8,128)(2,1)}) %all-gather.7.cloned.1.call-update) | async-done | bytes 4194320 | tf_op jit(solution)/shard_map/all_gather | solution.py:78
  123.4 5.8 %fusion.13 = (f32[768]{0:T(1024)S(1)}, f32[768,2048]{1,0:T(8,128)S(1)}) fusion(bf16[768,1024]{1,0:T(8,128)(2,1)} %fusion.2, bf16[1024,2048]{1,0:T(8,128)(2,1)} %all-gather.7.cloned.1.call-done), kind=kOutput, calls=%fused_computation.38 | convolution fusion | flops 3222797568 | bytes 12061696 | tf_op jit(solution)/shard_map/dot_general | solution.py:16
  129.2 2.0 exponential_reduce_fusion
  131.2 0.7 copy-done.1
  132.4 4.4 %multiply_convert_fusion = bf16[768,2048]{1,0:T(8,128)(2,1)S(1)} fusion(f32[768,2048]{1,0:T(8,128)} %copy-done.1, f32[768]{0:T(1024)S(1)} %get-tuple-element.13, f32[768]{0:T(1024)S(1)} %mul.90, s32[768]{0:T(1024)S(1)} %eq.29), kind=kLoop, calls=%fused_computation | loop fusion | flops 9437184 | bytes 9446400 | tf_op jit(solution)/shard_map/convert_element_type | solution.py:47
  136.9 1.7 copy-done.2
  138.6 3.5 fusion.4
  142.5 9.0 %fusion.14 = f32[1024,2048]{1,0:T(8,128)} fusion(bf16[768,1024]{0,1:T(8,128)(2,1)} %reshape.131, bf16[768,2048]{1,0:T(8,128)(2,1)} %copy-done.2), kind=kOutput, calls=%fused_computation.39 | convolution fusion | flops 3221225472 | bytes 13107200 | tf_op jit(solution)/shard_map/dot_general | solution.py:111
  151.5 0.6 fusion.10
  152.8 144.7 %all-reduce.5 = (f32[]{:T(128)}, bf16[1024,2048]{1,0:T(8,128)(2,1)}, bf16[1024]{0:T(1024)(128)(2,1)S(1)}) all-reduce(f32[]{:T(128)} %fusion.10, f32[1024,2048]{1,0:T(8,128)} %fusion.14, f32[1024]{0:T(1024)S(1)} %reshape.133), channel_id=1, replica_groups=mesh['wide'=32,'narrow'=8] {'wide','narrow'}, use_global_device_ids=true, to_apply=%region_6.7 | all-reduce | flops 2098177 | bytes 12589064 | tf_op jit(solution)/shard_map/psum | solution.py:103
  297.5 0.8 fusion.5
  298.4 0.2 dynamic-update-slice
  298.6 64.9 %all-reduce = bf16[128]{0:T(256)(128)(2,1)S(1)} all-reduce(bf16[128]{0:T(256)(128)(2,1)S(1)} %dynamic-update-slice), channel_id=1, replica_groups=mesh['wide'=32,'narrow'=8] {'wide'}, use_global_device_ids=true, to_apply=%add | all-reduce | flops 128 | bytes 512
  363.5 0.5 convert_element_type.49
  364.0 25.1 %all-gather.1 = bf16[32,4,2048]{2,1,0:T(4,128)(2,1)} all-gather(bf16[1,4,2048]{2,1,0:T(4,128)(2,1)S(1)} %fusion.5), channel_id=1, replica_groups=mesh['wide'=32,'narrow'=8] {'wide'}, dimensions={0}, use_global_device_ids=true | all-gather | bytes 540672 | tf_op jit(solution)/shard_map/all_gather | solution.py:120
  389.1 2.1 reshape.142
  (32 shorter events, 1.2 us)
Async XLA Ops:
  7.2 61.1 %copy-start = (bf16[1,1,3,2,128,2048]{5,4,3,2,1,0:T(8,128)(2,1)S(1)}, bf16[1,1,3,2,128,2048]{5,4,3,2,1,0:T(8,128)(2,1)}, u32[]{:S(2)}) copy-start(bf16[1,1,3,2,128,2048]{5,4,3,2,1,0:T(8,128)(2,1)} %param.9) | copy-start | bytes 9437188
  7.2 61.0 %all-gather.5.cloned.1.call-start = ((), (), s32[]{:S(2)}) async-start(), calls=%async_computation | async-start | bytes 4718592 | tf_op jit(solution)/shard_map/all_gather | solution.py:74
  7.9 115.4 %all-gather.7.cloned.1.call-start = ((), (), s32[]{:S(2)}) async-start(), calls=%async_computation.1 | async-start | bytes 4718592 | tf_op jit(solution)/shard_map/all_gather | solution.py:78
  73.9 1.2 copy-start.3
  129.2 2.7 copy-start.1
  132.4 6.2 %copy-start.4 = (bf16[768,1024]{1,0:T(8,128)(2,1)S(1)}, bf16[768,1024]{1,0:T(8,128)(2,1)}, u32[]{:S(2)}) copy-start(bf16[768,1024]{1,0:T(8,128)(2,1)} %copy-done.3) | copy-start | bytes 4718596
  132.4 6.2 %copy-start.7 = (bf16[1024,2048]{1,0:T(8,128)(2,1)S(1)}, bf16[1024,2048]{1,0:T(8,128)(2,1)}, u32[]{:S(2)}) copy-start(bf16[1024,2048]{1,0:T(8,128)(2,1)} %all-gather.7.cloned.1.call-done) | copy-start | bytes 12582916
  136.9 1.8 copy-start.2
  142.5 9.0 %copy-start.5 = (f32[1,1,3]{2,1,0:T(1,128)S(1)}, f32[1,1,3]{2,1,0:T(1,128)}, u32[]{:S(2)}) copy-start(f32[1,1,3]{2,1,0:T(1,128)} %param.13) | copy-start | bytes 40
  142.5 9.0 %copy-start.6 = (s32[1,1,3]{2,1,0:T(1,128)S(1)}, s32[1,1,3]{2,1,0:T(1,128)}, u32[]{:S(2)}) copy-start(s32[1,1,3]{2,1,0:T(1,128)} %param.12) | copy-start | bytes 40
Sparse Core Ops, SparseCore 0:
  9.8 58.3 all-gather.4
  70.0 53.3 all-gather.6
where the time goes:
time: 400 us
  blocking collectives  251 us (63%)
  waiting for transfers between devices  72.7 us (18%)
  local copies, waits for them, and re-layouts  24.3 us (6%)
  matrix products  24 us (6%)
  between operations  17.3 us (4%)
  other arithmetic  10.3 us (3%)
    psum x1, blocking collectives, on_device(): loss_sum = lax.psum(loss_part, ('wide', 'narrow'))  145 us
    unnamed x1, blocking collectives  64.9 us
    all_gather x1, waiting for transfers between devices, on_device(): lax.all_gather(proj_weight, 'narrow', axis=0, tiled=True)  38.3 us
    all_gather x1, waiting for transfers between devices, on_device(): lax.all_gather(head_weight, 'narrow', axis=0, tiled=True)  33.1 us
    all_gather x1, blocking collectives, on_device(): lax.all_gather(head_piece.astype(jnp.bfloat16), 'wide', axis=0, tiled=True)  25.1 us
    all_gather x1, blocking collectives, on_device(): lax.all_gather(norm_gain, 'narrow', axis=0, tiled=True)  16.4 us
    dot_general x1, matrix products, on_device(): jnp.dot(normed_order.T, dlogits, preferred_element_type=jnp.float32)  9.01 us
  transfers between devices with their start and end apart: 2, of which 2 were waited for; matrix products, arithmetic and copies ran while one was open for 6% of the time, Pallas kernels for 0%

commit v1 on v0

--- a/solution.py
+++ b/solution.py
@@ -5,6 +5,11 @@
 
 norm_eps = 1e-06
 margin_scale = 2.0
+
+
+def gather_over(array, axis, dim):
+    sent = jnp.stack([array] * lax.axis_size(axis))
+    return jnp.concatenate(lax.all_to_all(sent, axis, 0, 0), axis=dim)
 
 
 def forward_terms(projected, codes, lengths, live_pairs, gain_full, head_full):
@@ -117,9 +122,7 @@
         lax.psum_scatter(gain_order, ("wide", "narrow"), scatter_dimension=0, tiled=True),
     )
     grad_head, grad_gain = (
-        lax.all_gather(head_piece.astype(jnp.bfloat16), "wide", axis=0, tiled=True).astype(
-            head_piece.dtype
-        ),
+        gather_over(head_piece.astype(jnp.bfloat16), "wide", 0).astype(head_piece.dtype),
         lax.all_gather(gain_piece.astype(jnp.bfloat16), "wide", axis=0, tiled=True).astype(
             gain_piece.dtype
         ),

time: 400 us -> 385 us (0.963)
  blocking collectives: 251 us -> 225 us
  starting transfers between devices: 0.08 us -> 7.13 us
    all_gather x1 -> x0, blocking collectives: 25.1 us -> none  [on_device(): lax.all_gather(head_piece.astype(jnp.bfloat16), 'wide', axis=0, tiled=True)]
    all_to_all x0 -> x1, starting transfers between devices: none -> 7.05 us  [gather_over(): return jnp.concatenate(lax.all_to_all(sent, axis, 0, 0), axis=dim)]
  transfers between devices with their start and end apart: 2 -> 3, of which waited for: 2 -> 2; matrix products, arithmetic and copies ran while one was open for 6% -> 7% of each run, Pallas kernels for 0% -> 0%
where the time goes in v1:
time: 385 us; the launch traced here: 383 us
  blocking collectives  225 us (58%)
  waiting for transfers between devices  74 us (19%)
  local copies, waits for them, and re-layouts  24.6 us (6%)
  matrix products  24 us (6%)
  between operations  17.3 us (4%)
  other arithmetic  10.3 us (3%)
  starting transfers between devices  7.13 us (2%)
    psum x1, blocking collectives, on_device(): loss_sum = lax.psum(loss_part, ('wide', 'narrow'))  145 us
    unnamed x1, blocking collectives  64.3 us
    all_gather x1, waiting for transfers between devices, on_device(): lax.all_gather(proj_weight, 'narrow', axis=0, tiled=True)  39.5 us
    all_gather x1, waiting for transfers between devices, on_device(): lax.all_gather(head_weight, 'narrow', axis=0, tiled=True)  33.1 us
    all_gather x1, blocking collectives, on_device(): lax.all_gather(norm_gain, 'narrow', axis=0, tiled=True)  16.4 us
    dot_general x1, matrix products, on_device(): jnp.dot(normed_order.T, dlogits, preferred_element_type=jnp.float32)  9.01 us
  transfers between devices with their start and end apart: 3, of which 2 were waited for; matrix products, arithmetic and copies ran while one was open for 7% of the time, Pallas kernels for 0%

profile of v1, /device:TPU:1, one launch (start us, length us, event | category | flops | bytes accessed | tf_op | source)
XLA Modules:
  0.0 382.7 jit_solution(4015921430239310383)
XLA Ops:
  7.2 0.7 all-gather.4.cloned.1.call-update
  8.0 0.7 all-gather.6.cloned.1.call-update
  9.3 0.7 compare_bitcast_fusion
  10.1 0.8 copy.33
  10.9 0.7 copy.39
  11.6 0.7 eq.29
  12.3 16.4 %all-gather = bf16[8,1,128]{2,1,0:T(2,128)(2,1)S(1)} all-gather(bf16[1,1,128]{2,1,0:T(2,128)(2,1)} %bitcast.51), channel_id=1, replica_groups=mesh['wide'=32,'narrow'=8] {'narrow'}, dimensions={0}, use_global_device_ids=true | all-gather | bytes 2304 | tf_op jit(solution)/shard_map/all_gather | solution.py:84
  28.7 39.5 %all-gather.4.cloned.1.call-done = bf16[2048,1024]{1,0:T(8,128)(2,1)} async-done(((bf16[256,1024]{1,0:T(8,128)(2,1)}), bf16[2048,1024]{1,0:T(8,128)(2,1)}) %all-gather.4.cloned.1.call-update) | async-done | bytes 4194320 | tf_op jit(solution)/shard_map/all_gather | solution.py:79
  68.2 5.7 %fusion = (f32[768]{0:T(1024)S(1)}, bf16[768,1024]{1,0:T(8,128)(2,1)S(1)}) fusion(bf16[768,2048]{1,0:T(8,128)(2,1)S(1)} %bitcast.45, bf16[2048,1024]{1,0:T(8,128)(2,1)} %all-gather.4.cloned.1.call-done), kind=kOutput, calls=%fused_computation.7 | convolution fusion | flops 3224370432 | bytes 8915968 | tf_op jit(solution)/shard_map/dot_general | solution.py:77
  73.9 1.1 copy-done.3
  75.0 1.6 fusion.2
  76.6 2.6 copy.35
  79.2 3.9 %reshape.135 = bf16[768,8,32,4]{0,3,2,1:T(4,128)(2,1)} reshape(bf16[768,1024]{0,1:T(8,128)(2,1)} %copy.35) | data formatting | bytes 3145728 | tf_op jit(solution)/shard_map/reshape | solution.py:112
  83.1 3.4 copy.36
  86.5 3.8 reshape.136
  90.3 33.1 %all-gather.6.cloned.1.call-done = bf16[1024,2048]{1,0:T(8,128)(2,1)} async-done(((bf16[128,2048]{1,0:T(8,128)(2,1)}), bf16[1024,2048]{1,0:T(8,128)(2,1)}) %all-gather.6.cloned.1.call-update) | async-done | bytes 4194320 | tf_op jit(solution)/shard_map/all_gather | solution.py:83
  123.4 5.8 %fusion.12 = (f32[768]{0:T(1024)S(1)}, f32[768,2048]{1,0:T(8,128)S(1)}) fusion(bf16[768,1024]{1,0:T(8,128)(2,1)} %fusion.2, bf16[1024,2048]{1,0:T(8,128)(2,1)} %all-gather.6.cloned.1.call-done), kind=kOutput, calls=%fused_computation.37 | convolution fusion | flops 3222797568 | bytes 12061696 | tf_op jit(solution)/shard_map/dot_general | solution.py:21
  129.2 2.0 exponential_reduce_fusion
  131.2 0.7 copy-done.1
  132.4 4.4 %multiply_convert_fusion = bf16[768,2048]{1,0:T(8,128)(2,1)S(1)} fusion(f32[768,2048]{1,0:T(8,128)} %copy-done.1, f32[768]{0:T(1024)S(1)} %get-tuple-element.13, f32[768]{0:T(1024)S(1)} %mul.90, s32[768]{0:T(1024)S(1)} %eq.29), kind=kLoop, calls=%fused_computation | loop fusion | flops 9437184 | bytes 9446400 | tf_op jit(solution)/shard_map/convert_element_type | solution.py:52
  136.9 1.7 copy-done.2
  138.6 3.5 fusion.4
  142.5 9.0 %fusion.13 = f32[1024,2048]{1,0:T(8,128)} fusion(bf16[768,1024]{0,1:T(8,128)(2,1)} %reshape.136, bf16[768,2048]{1,0:T(8,128)(2,1)} %copy-done.2), kind=kOutput, calls=%fused_computation.38 | convolution fusion | flops 3221225472 | bytes 13107200 | tf_op jit(solution)/shard_map/dot_general | solution.py:116
  151.5 0.6 fusion.9
  152.1 144.7 %all-reduce.5 = (f32[]{:T(128)}, bf16[1024,2048]{1,0:T(8,128)(2,1)}, bf16[1024]{0:T(1024)(128)(2,1)S(1)}) all-reduce(f32[]{:T(128)} %fusion.9, f32[1024,2048]{1,0:T(8,128)} %fusion.13, f32[1024]{0:T(1024)S(1)} %reshape.138), channel_id=1, replica_groups=mesh['wide'=32,'narrow'=8] {'wide','narrow'}, use_global_device_ids=true, to_apply=%region_6.7 | all-reduce | flops 2098177 | bytes 12589064 | tf_op jit(solution)/shard_map/psum | solution.py:108
  296.9 0.8 dynamic-slice_convert_fusion
  297.6 1.0 stack.5
  298.7 7.1 %all-to-all-start = ((bf16[32,4,2048]{2,1,0:T(4,128)(2,1)}), bf16[32,4,2048]{2,1,0:T(4,128)(2,1)}, u32[]{:S(2)}, u32[]{:S(2)}) async-start(bf16[32,4,2048]{2,1,0:T(4,128)(2,1)} %stack.5), calls=%async_computation | async-start | bytes 1048576 | tf_op jit(solution)/shard_map/all_to_all | solution.py:12
  305.7 0.6 dynamic-slice
  307.2 64.3 %all-reduce = bf16[128]{0:T(256)(128)(2,1)S(1)} all-reduce(bf16[128]{0:T(256)(128)(2,1)S(1)} %dynamic-update-slice), channel_id=1, replica_groups=mesh['wide'=32,'narrow'=8] {'wide'}, use_global_device_ids=true, to_apply=%add | all-reduce | flops 128 | bytes 512
  371.5 0.5 convert_element_type.53
  372.7 2.1 reshape.139
  (36 shorter events, 1.4 us)
Async XLA Ops:
  7.2 61.1 %copy-start = (bf16[1,1,3,2,128,2048]{5,4,3,2,1,0:T(8,128)(2,1)S(1)}, bf16[1,1,3,2,128,2048]{5,4,3,2,1,0:T(8,128)(2,1)}, u32[]{:S(2)}) copy-start(bf16[1,1,3,2,128,2048]{5,4,3,2,1,0:T(8,128)(2,1)} %param.9) | copy-start | bytes 9437188
  7.2 61.0 %all-gather.4.cloned.1.call-start = ((), (), s32[]{:S(2)}) async-start(), calls=%async_computation.1 | async-start | bytes 4718592 | tf_op jit(solution)/shard_map/all_gather | solution.py:79
  7.9 115.4 %all-gather.6.cloned.1.call-start = ((), (), s32[]{:S(2)}) async-start(), calls=%async_computation.2 | async-start | bytes 4718592 | tf_op jit(solution)/shard_map/all_gather | solution.py:83
  73.9 1.2 copy-start.3
  129.2 2.7 copy-start.1
  132.4 6.2 %copy-start.4 = (bf16[768,1024]{1,0:T(8,128)(2,1)S(1)}, bf16[768,1024]{1,0:T(8,128)(2,1)}, u32[]{:S(2)}) copy-start(bf16[768,1024]{1,0:T(8,128)(2,1)} %copy-done.3) | copy-start | bytes 4718596
  132.4 6.2 %copy-start.7 = (bf16[1024,2048]{1,0:T(8,128)(2,1)S(1)}, bf16[1024,2048]{1,0:T(8,128)(2,1)}, u32[]{:S(2)}) copy-start(bf16[1024,2048]{1,0:T(8,128)(2,1)} %all-gather.6.cloned.1.call-done) | copy-start | bytes 12582916
  136.9 1.8 copy-start.2
  142.5 9.0 %copy-start.5 = (f32[1,1,3]{2,1,0:T(1,128)S(1)}, f32[1,1,3]{2,1,0:T(1,128)}, u32[]{:S(2)}) copy-start(f32[1,1,3]{2,1,0:T(1,128)} %param.13) | copy-start | bytes 40
  142.5 9.0 %copy-start.6 = (s32[1,1,3]{2,1,0:T(1,128)S(1)}, s32[1,1,3]{2,1,0:T(1,128)}, u32[]{:S(2)}) copy-start(s32[1,1,3]{2,1,0:T(1,128)} %param.12) | copy-start | bytes 40
  152.1 153.6 %copy-start.8 = (u32[256]{0:T(256)S(1)}, u32[256]{0:T(256)}, u32[]{:S(2)}) copy-start(u32[256]{0:T(256)} %constant.35) | copy-start | bytes 3076
  298.7 74.0 %all-to-all-start = ((bf16[32,4,2048]{2,1,0:T(4,128)(2,1)}), bf16[32,4,2048]{2,1,0:T(4,128)(2,1)}, u32[]{:S(2)}, u32[]{:S(2)}) async-start(bf16[32,4,2048]{2,1,0:T(4,128)(2,1)} %stack.5), calls=%async_computation | async-start | bytes 1048576 | tf_op jit(solution)/shard_map/all_to_all | solution.py:12
Sparse Core Ops, SparseCore 0:
  9.8 58.3 all-gather.3
  70.0 53.3 all-gather.5
